TPU v7x, 512 devices: a whole 4x8x8 slice. The times are simulated.
512 devices in a mesh: req: 64 (over z_lo, x, y), tp: 8 (over z_hi, core).
Axes of the slice: x: 4, y: 8, z: 8 (z_hi: 4, z_lo: 2; z = z_hi * 2 + z_lo), core: 2. Of those that a mesh axis runs over, the one named last changes fastest.
Arguments:
- q_proj: bfloat16 [64, 128, 3072], P('req', None, 'tp'), may hold values from -24 to 24, as said below
- kv_proj: bfloat16 [64, 128, 2, 1024], P('req', None, None, 'tp'), may hold values from -6 to 6
- q_bias: bfloat16 [3072], P('tp'), may hold values from -3 to 3
- kv_bias: bfloat16 [2, 1024], P(None, 'tp'), may hold values from -3 to 3
- prefix_kv: bfloat16 [64, 1024, 2, 1024], P('req', None, None, 'tp'), may hold values from -24 to 24, as said below
- lengths: int32 [64], P('req'), may hold values from 1 to 128, 4096 in all
- group_of: int32 [64], P('req'), may hold values from 0 to 2
- owner: int32 [3], replicated, may hold values from 0 to 63
- positions: int32 [64, 128], P('req'), may hold values from 1024 to 1278, as said below
- residual: bfloat16 [64, 128, 5120], P('req', None, 'tp'), may hold values from -6 to 6
- out_weight: bfloat16 [3072, 5120], P(None, 'tp'), may hold values from -0.109375 to 0.109375
Outputs:
- hidden: bfloat16 [64, 128, 5120], P('req', None, 'tp')
Inputs may be any that keep to these rules, and one draw needn't show every extreme that they name: `q_proj`: projected queries; entries stay within the stated bounds. `prefix_kv`: cached keys are already rotated at prefix positions 0 to 1023. Each request's positions are a start of 1024 or more plus the slot index.
All inputs are finite; a program needn't handle non-finite values. No bound on the sum of `lengths` on one device may be relied on, other than what follows from the above.
Results may differ from a plain program's by a relative error of at most 0.006.
Values may be sent and summed in bfloat16 or wider, within the bound.
No kernel may reach another device: no remote copies, remote signals or barrier semaphores. Data moves between devices by JAX's collectives and lax.ppermute only.
A program may use at most 128 MiB of HBM per device.

v0:
```python
import math
import jax
import jax.numpy as jnp
from jax import lax
from jax.sharding import PartitionSpec as P

HD = 128


def rotate(vectors, places):
    half = HD // 2
    index = jnp.arange(half).astype(jnp.float32)
    freqs = jnp.exp(index * (-2.0 / HD) * math.log(1000000.0))
    angles = places.astype(jnp.float32)[:, None] * freqs[None, :]
    cosine = jnp.concatenate([jnp.cos(angles), jnp.cos(angles)], axis=-1)[:, None, :]
    sine = jnp.concatenate([jnp.sin(angles), jnp.sin(angles)], axis=-1)[:, None, :]
    turned = jnp.concatenate([-vectors[..., half:], vectors[..., :half]], axis=-1)
    return vectors * cosine + turned * sine


def fetch_prefix(slab, group, owner):
    columns = lax.axis_size("req")
    piece = slab.shape[0] // columns
    pieces = slab.reshape(columns, piece, 2, HD)
    tag = jnp.broadcast_to(group.astype(slab.dtype), (columns, 1, 2, HD))
    spread = lax.all_to_all(jnp.concatenate([pieces, tag], axis=1), "req", 0, 0, tiled=True)
    groups = spread[:, piece, 0, 0].astype(jnp.int32)
    owned = [
        jnp.swapaxes(lax.dynamic_index_in_dim(spread, owner[g], 0, keepdims=False)[:piece], 0, 1)
        for g in range(owner.shape[0])
    ]
    outgoing = jnp.broadcast_to(owned[0], (columns, 2, piece, HD))
    for g in range(1, owner.shape[0]):
        outgoing = jnp.where((groups == g)[:, None, None, None], owned[g][None], outgoing)
    return lax.all_to_all(outgoing, "req", 0, 0, tiled=True)


def attend_rows(queries, all_keys, all_vals, length, prefix_len):
    count = queries.shape[0]
    slots = jnp.arange(count)
    causal = slots[None, :] <= slots[:, None]
    allowed = jnp.concatenate([jnp.ones((count, prefix_len), dtype=bool), causal], axis=1)
    scores = jnp.einsum("rhd,kd->hrk", queries, all_keys, preferred_element_type=jnp.float32) * (
        1.0 / math.sqrt(HD)
    )
    scores = jnp.where(allowed[None], scores, -1e30)
    top = jnp.max(scores, axis=-1, keepdims=True)
    weights = jnp.where(allowed[None], jnp.exp(scores - top), 0.0)
    total = jnp.sum(weights, axis=-1)
    rounded = weights.astype(jnp.bfloat16)
    mixed = jnp.einsum("hrk,kd->rhd", rounded, all_vals, preferred_element_type=jnp.float32)
    mixed = mixed / jnp.transpose(total)[:, :, None]
    mixed = jnp.where((slots < length)[:, None, None], mixed, 0.0)
    return mixed.astype(jnp.bfloat16)


def body(
    q_proj,
    kv_proj,
    q_bias,
    kv_bias,
    prefix_kv,
    lengths,
    group_of,
    owner,
    positions,
    residual,
    out_weight,
):
    cap = q_proj.shape[1]
    prefix_len = prefix_kv.shape[1]
    length = lengths[0]
    places = positions[0]
    slab = fetch_prefix(prefix_kv[0], group_of[0], owner)
    queries = q_proj[0].astype(jnp.float32).reshape(cap, -1, HD) + q_bias.astype(
        jnp.float32
    ).reshape(-1, HD)
    queries = rotate(queries, places).astype(jnp.bfloat16)
    pairs = kv_proj[0].astype(jnp.float32) + kv_bias.astype(jnp.float32)
    keys = rotate(pairs[:, 0][:, None, :], places)[:, 0].astype(jnp.bfloat16)
    vals = pairs[:, 1].astype(jnp.bfloat16)
    all_keys = jnp.concatenate([slab[:, 0].reshape(prefix_len, HD), keys], axis=0)
    all_vals = jnp.concatenate([slab[:, 1].reshape(prefix_len, HD), vals], axis=0)
    attended = attend_rows(queries, all_keys, all_vals, length, prefix_len)
    attended = attended.reshape(cap, -1)
    whole_heads = lax.all_gather(attended, "tp", axis=1, tiled=True)
    projected = jnp.dot(whole_heads, out_weight, preferred_element_type=jnp.float32)
    hidden = (residual[0].astype(jnp.float32) + projected).astype(jnp.bfloat16)
    return hidden[None]


def solution(mesh):
    in_specs = (
        P("req", None, "tp"),
        P("req", None, None, "tp"),
        P("tp"),
        P(None, "tp"),
        P("req", None, None, "tp"),
        P("req"),
        P("req"),
        P(),
        P("req", None),
        P("req", None, "tp"),
        P(None, "tp"),
    )
    out_specs = P("req", None, "tp")
    return jax.shard_map(body, mesh=mesh, in_specs=in_specs, out_specs=out_specs, check_vma=False)
```

profile of v0, /device:TPU:1, one launch (start us, length us, event | category | flops | bytes accessed | tf_op | source)
XLA Modules:
  0.0 89.6 jit_solution(15967355962080478842)
XLA Ops:
  0.0 1.1 %copy.38 = bf16[1,1024,2,128]{3,1,2,0:T(8,128)(2,1)S(1)} copy(bf16[1,1024,2,128]{3,2,1,0:T(2,128)(2,1)} %param.15) | data formatting | bytes 1048576 | tf_op args[4]
  1.2 0.5 copy.61
  2.4 1.2 %concatenate.45.clone = bf16[64,17,2,128]{3,2,1,0:T(2,128)(2,1)} pad(bf16[64,16,2,128]{3,2,1,0:T(2,128)(2,1)S(1)} %copy.61, bf16[]{:T(256)} %bitcast.3), padding=0_0x0_1x0_0x0_0 | pad | bytes 1081346 | tf_op jit(solution)/shard_map/concatenate | solution.py:26
  3.6 12.9 %all-to-all-start = ((bf16[64,17,2,128]{3,2,1,0:T(2,128)(2,1)}), bf16[64,17,2,128]{3,2,1,0:T(2,128)(2,1)S(1)}, u32[]{:S(2)}, u32[]{:S(2)}) async-start(bf16[64,17,2,128]{3,2,1,0:T(2,128)(2,1)} %concatenate.45.clone), calls=%async_computation | async-start | bytes 1114112 | tf_op jit(solution)/shard_map/all_to_all | solution.py:26
  16.5 0.6 fusion.32
  21.1 0.1 copy.46
  21.2 0.1 copy.47
  21.3 0.3 fusion.22
  21.6 0.1 pad_maximum_fusion
  21.8 0.1 copy.48
  24.7 9.1 %all-to-all-done = bf16[64,17,2,128]{3,2,1,0:T(2,128)(2,1)S(1)} async-done(((bf16[64,17,2,128]{3,2,1,0:T(2,128)(2,1)}), bf16[64,17,2,128]{3,2,1,0:T(2,128)(2,1)S(1)}, u32[]{:S(2)}, u32[]{:S(2)}) %all-to-all-start) | async-done | bytes 557088 | tf_op jit(solution)/shard_map/all_to_all | solution.py:26
  33.8 2.4 %compare_reduce_fusion.1 = (pred[64]{0:T(512)(128)(4,1)S(1)}, pred[64]{0:T(512)(128)(4,1)S(1)}) fusion(bf16[64,17,2,128]{3,2,1,0:T(2,128)(2,1)S(1)} %all-to-all-done), kind=kLoop, calls=%fused_computation.28 | loop fusion | flops 192 | bytes 256 | tf_op jit(solution)/shard_map/eq | solution.py:34
  36.2 1.0 %select_select_fusion = bf16[64,2,16,128]{3,2,1,0:T(8,128)(2,1)} fusion(pred[64]{0:T(512)(128)(4,1)S(1)} %get-tuple-element.6, pred[64]{0:T(512)(128)(4,1)S(1)} %get-tuple-element.5, bf16[2,16,128]{2,1,0:T(8,128)(2,1)S(1)} %get-tuple-element.22, bf16[2,16,128]{2,1,0:T(8,128)(2,1)S(1)} %get-tuple-element.23, bf16[2,16,128]{2,1,0:T(8,128)(2,1)S(1)} %bitcast.89), kind=kLoop, calls=%fused_computation.15 | loop fusion | flops 524288 | bytes 548992 | tf_op jit(solution)/shard_map/jit(_where)/select_n | solution.py:34
  37.2 6.3 %all-to-all-start.1 = ((bf16[64,2,16,128]{3,2,1,0:T(8,128)(2,1)}), bf16[64,2,16,128]{3,2,1,0:T(8,128)(2,1)S(1)}, u32[]{:S(2)}, u32[]{:S(2)}) async-start(bf16[64,2,16,128]{3,2,1,0:T(8,128)(2,1)} %select_select_fusion), calls=%async_computation.1 | async-start | bytes 1048576 | tf_op jit(solution)/shard_map/all_to_all | solution.py:35
  43.5 0.1 fusion.21
  43.6 0.1 convert_add_fusion
  43.8 0.1 fusion.17
  43.9 15.3 %all-to-all-done.1 = bf16[64,2,16,128]{3,2,1,0:T(8,128)(2,1)S(1)} async-done(((bf16[64,2,16,128]{3,2,1,0:T(8,128)(2,1)}), bf16[64,2,16,128]{3,2,1,0:T(8,128)(2,1)S(1)}, u32[]{:S(2)}, u32[]{:S(2)}) %all-to-all-start.1) | async-done | bytes 524320 | tf_op jit(solution)/shard_map/all_to_all | solution.py:35
  59.2 0.4 fusion.3
  59.7 0.9 %fusion.33 = f32[3,128]{1,0:T(4,128)S(1)} fusion(bf16[128,3,128]{0,2,1:T(8,128)(2,1)S(1)} %fusion.17, pred[128,1152]{0,1:T(8,128)(4,1)S(1)} %concatenate.47, bf16[128,128]{1,0:T(8,128)(2,1)S(1)} %fusion.21, bf16[1024,128]{1,0:T(8,128)(2,1)S(1)} %bitcast.84), kind=kOutput, calls=%fused_computation.64 | convolution fusion | flops 116049024 | bytes 542208 | tf_op jit(solution)/shard_map/sub | solution.py:48
  60.6 0.1 copy.45
  60.7 0.6 fusion.10
  61.4 24.6 %all_gather.3 = bf16[128,3072]{0,1:T(8,128)(2,1)S(1)} all-gather(bf16[128,384]{0,1:T(8,128)(2,1)S(1)} %bitcast.88), channel_id=1, replica_groups=mesh['req'=64,'tp'=8] {'tp'}, dimensions={1}, use_global_device_ids=true | all-gather | bytes 884736 | tf_op jit(solution)/shard_map/all_gather | solution.py:86
  85.9 3.6 %fusion.9 = bf16[1,128,640]{2,1,0:T(8,128)(2,1)} fusion(bf16[128,3072]{0,1:T(8,128)(2,1)S(1)} %all_gather.3, bf16[3072,640]{1,0:T(8,128)(2,1)} %param.21, bf16[1,128,640]{2,1,0:T(8,128)(2,1)S(1)} %copy-done), kind=kOutput, calls=%fused_computation.12 | convolution fusion | flops 503562240 | bytes 5046272 | tf_op jit(solution)/shard_map/dot_general | solution.py:87
  (30 shorter events, 0.4 us)
Async XLA Ops:
  1.1 15.4 %copy-start.3 = (s32[3]{0:T(128)S(1)}, s32[3]{0:T(128)}, u32[]{:S(2)}) copy-start(s32[3]{0:T(128)} %param.18) | copy-start | bytes 40
  1.1 19.9 %copy-start.5 = (bf16[2,128]{1,0:T(2,128)(2,1)S(1)}, bf16[2,128]{1,0:T(2,128)(2,1)}, u32[]{:S(2)}) copy-start(bf16[2,128]{1,0:T(2,128)(2,1)} %param.14) | copy-start | bytes 1540
  1.1 19.9 %copy-start.2 = (bf16[1,128,2,128]{3,2,1,0:T(2,128)(2,1)S(1)}, bf16[1,128,2,128]{3,2,1,0:T(2,128)(2,1)}, u32[]{:S(2)}) copy-start(bf16[1,128,2,128]{3,2,1,0:T(2,128)(2,1)} %param.12) | copy-start | bytes 196612
  1.1 20.0 %copy-start.1 = (bf16[1,128,384]{2,1,0:T(8,128)(2,1)S(1)}, bf16[1,128,384]{2,1,0:T(8,128)(2,1)}, u32[]{:S(2)}) copy-start(bf16[1,128,384]{2,1,0:T(8,128)(2,1)} %param.11) | copy-start | bytes 294916
  1.2 20.1 %copy-start.6 = (s32[1,128]{1,0:T(1,128)S(1)}, s32[1,128]{1,0:T(1,128)}, u32[]{:S(2)}) copy-start(s32[1,128]{1,0:T(1,128)} %param.19) | copy-start | bytes 1540
  2.4 22.2 %copy-start.4 = (bf16[384]{0:T(512)(128)(2,1)S(1)}, bf16[384]{0:T(512)(128)(2,1)}, u32[]{:S(2)}) copy-start(bf16[384]{0:T(512)(128)(2,1)} %param.13) | copy-start | bytes 2308
  3.6 30.2 %all-to-all-start = ((bf16[64,17,2,128]{3,2,1,0:T(2,128)(2,1)}), bf16[64,17,2,128]{3,2,1,0:T(2,128)(2,1)S(1)}, u32[]{:S(2)}, u32[]{:S(2)}) async-start(bf16[64,17,2,128]{3,2,1,0:T(2,128)(2,1)} %concatenate.45.clone), calls=%async_computation | async-start | bytes 1114112 | tf_op jit(solution)/shard_map/all_to_all | solution.py:26
  37.2 22.0 %all-to-all-start.1 = ((bf16[64,2,16,128]{3,2,1,0:T(8,128)(2,1)}), bf16[64,2,16,128]{3,2,1,0:T(8,128)(2,1)S(1)}, u32[]{:S(2)}, u32[]{:S(2)}) async-start(bf16[64,2,16,128]{3,2,1,0:T(8,128)(2,1)} %select_select_fusion), calls=%async_computation.1 | async-start | bytes 1048576 | tf_op jit(solution)/shard_map/all_to_all | solution.py:35
  60.7 25.2 %copy-start = (bf16[1,128,640]{2,1,0:T(8,128)(2,1)S(1)}, bf16[1,128,640]{2,1,0:T(8,128)(2,1)}, u32[]{:S(2)}) copy-start(bf16[1,128,640]{2,1,0:T(8,128)(2,1)} %param.20) | copy-start | bytes 491524
where the time goes:
time: 90 us; the launch traced here: 89.6 us
  blocking collectives  24.6 us (27%)
  waiting for transfers between devices  24.4 us (27%)
  starting transfers between devices  19.2 us (21%)
  between operations  7.34 us (8%)
  matrix products  5.58 us (6%)
  other arithmetic  4.3 us (5%)
  local copies, waits for them, and re-layouts  4.2 us (5%)
    all_gather x1, blocking collectives, body(): whole_heads = lax.all_gather(attended, 'tp', axis=1, tiled=True)  24.6 us
    all_to_all x1, waiting for transfers between devices, fetch_prefix(): return lax.all_to_all(outgoing, 'req', 0, 0, tiled=True)  15.3 us
    all_to_all x1, starting transfers between devices, fetch_prefix(): lax.all_to_all(jnp.concatenate([pieces, tag], axis=1), 'req', 0, 0, tiled...  12.9 us
    all_to_all x1, waiting for transfers between devices, fetch_prefix(): lax.all_to_all(jnp.concatenate([pieces, tag], axis=1), 'req', 0, 0, tiled...  9.09 us
    all_to_all x1, starting transfers between devices, fetch_prefix(): return lax.all_to_all(outgoing, 'req', 0, 0, tiled=True)  6.25 us
    dot_general x1, matrix products, body(): jnp.dot(whole_heads, out_weight, preferred_element_type=jnp.float32)  3.62 us
    eq x1, other arithmetic, fetch_prefix(): groups == g  2.39 us
    unnamed x18, local copies, waits for them, and re-layouts  1.82 us
  transfers between devices with their start and end apart: 2, of which 2 were waited for; matrix products, arithmetic and copies ran while one was open for 2% of the time, Pallas kernels for 0%

commit v1 on v0

--- a/solution.py
+++ b/solution.py
@@ -83,7 +83,8 @@
     all_vals = jnp.concatenate([slab[:, 1].reshape(prefix_len, HD), vals], axis=0)
     attended = attend_rows(queries, all_keys, all_vals, length, prefix_len)
     attended = attended.reshape(cap, -1)
-    whole_heads = lax.all_gather(attended, "tp", axis=1, tiled=True)
+    sent = jnp.stack([attended] * lax.axis_size("tp"))
+    whole_heads = jnp.concatenate(lax.all_to_all(sent, "tp", 0, 0), axis=1)
     projected = jnp.dot(whole_heads, out_weight, preferred_element_type=jnp.float32)
     hidden = (residual[0].astype(jnp.float32) + projected).astype(jnp.bfloat16)
     return hidden[None]

time: 90 us -> 100 us (1.11)
  the two profiles are of different devices: /device:TPU:1 before, /device:TPU:2 now
where the time goes in v1:
time: 100 us; the launch traced here: 99.9 us
  blocking collectives  33.2 us (33%)
  waiting for transfers between devices  26.8 us (27%)
  starting transfers between devices  18.4 us (18%)
  between operations  7.35 us (7%)
  matrix products  5.57 us (6%)
  local copies, waits for them, and re-layouts  4.3 us (4%)
  other arithmetic  4.3 us (4%)
    all_to_all x1, blocking collectives, body(): whole_heads = jnp.concatenate(lax.all_to_all(sent, 'tp', 0, 0), axis=1)  33.2 us
    all_to_all x1, waiting for transfers between devices, fetch_prefix(): return lax.all_to_all(outgoing, 'req', 0, 0, tiled=True)  16.4 us
    all_to_all x1, starting transfers between devices, fetch_prefix(): lax.all_to_all(jnp.concatenate([pieces, tag], axis=1), 'req', 0, 0, tiled...  12.5 us
    all_to_all x1, waiting for transfers between devices, fetch_prefix(): lax.all_to_all(jnp.concatenate([pieces, tag], axis=1), 'req', 0, 0, tiled...  10.3 us
    all_to_all x1, starting transfers between devices, fetch_prefix(): return lax.all_to_all(outgoing, 'req', 0, 0, tiled=True)  5.96 us
    dot_general x1, matrix products, body(): jnp.dot(whole_heads, out_weight, preferred_element_type=jnp.float32)  3.62 us
    eq x1, other arithmetic, fetch_prefix(): groups == g  2.39 us
  transfers between devices with their start and end apart: 2, of which 2 were waited for; matrix products, arithmetic and copies ran while one was open for 2% of the time, Pallas kernels for 0%

profile of v1, /device:TPU:2, one launch (start us, length us, event | category | flops | bytes accessed | tf_op | source)
XLA Modules:
  0.0 99.9 jit_solution(3016820370294271889)
XLA Ops:
  0.0 1.1 %copy.39 = bf16[1,1024,2,128]{3,1,2,0:T(8,128)(2,1)S(1)} copy(bf16[1,1024,2,128]{3,2,1,0:T(2,128)(2,1)} %param.15) | data formatting | bytes 1048576 | tf_op args[4]
  1.2 0.5 copy.62
  2.4 1.2 %concatenate.45.clone = bf16[64,17,2,128]{3,2,1,0:T(2,128)(2,1)} pad(bf16[64,16,2,128]{3,2,1,0:T(2,128)(2,1)S(1)} %copy.62, bf16[]{:T(256)} %bitcast.3), padding=0_0x0_1x0_0x0_0 | pad | bytes 1081346 | tf_op jit(solution)/shard_map/concatenate | solution.py:26
  3.6 12.5 %all-to-all-start = ((bf16[64,17,2,128]{3,2,1,0:T(2,128)(2,1)}), bf16[64,17,2,128]{3,2,1,0:T(2,128)(2,1)S(1)}, u32[]{:S(2)}, u32[]{:S(2)}) async-start(bf16[64,17,2,128]{3,2,1,0:T(2,128)(2,1)} %concatenate.45.clone), calls=%async_computation | async-start | bytes 1114112 | tf_op jit(solution)/shard_map/all_to_all | solution.py:26
  16.1 0.6 fusion.32
  20.6 0.1 copy.47
  20.7 0.1 copy.48
  20.9 0.3 fusion.22
  21.2 0.1 pad_maximum_fusion
  24.2 10.3 %all-to-all-done = bf16[64,17,2,128]{3,2,1,0:T(2,128)(2,1)S(1)} async-done(((bf16[64,17,2,128]{3,2,1,0:T(2,128)(2,1)}), bf16[64,17,2,128]{3,2,1,0:T(2,128)(2,1)S(1)}, u32[]{:S(2)}, u32[]{:S(2)}) %all-to-all-start) | async-done | bytes 557088 | tf_op jit(solution)/shard_map/all_to_all | solution.py:26
  34.6 2.4 %compare_reduce_fusion.1 = (pred[64]{0:T(512)(128)(4,1)S(1)}, pred[64]{0:T(512)(128)(4,1)S(1)}) fusion(bf16[64,17,2,128]{3,2,1,0:T(2,128)(2,1)S(1)} %all-to-all-done), kind=kLoop, calls=%fused_computation.28 | loop fusion | flops 192 | bytes 256 | tf_op jit(solution)/shard_map/eq | solution.py:34
  37.0 1.0 %select_select_fusion = bf16[64,2,16,128]{3,2,1,0:T(8,128)(2,1)} fusion(pred[64]{0:T(512)(128)(4,1)S(1)} %get-tuple-element.6, pred[64]{0:T(512)(128)(4,1)S(1)} %get-tuple-element.5, bf16[2,16,128]{2,1,0:T(8,128)(2,1)S(1)} %get-tuple-element.22, bf16[2,16,128]{2,1,0:T(8,128)(2,1)S(1)} %get-tuple-element.23, bf16[2,16,128]{2,1,0:T(8,128)(2,1)S(1)} %bitcast.93), kind=kLoop, calls=%fused_computation.15 | loop fusion | flops 524288 | bytes 548992 | tf_op jit(solution)/shard_map/jit(_where)/select_n | solution.py:34
  38.0 6.0 %all-to-all-start.1 = ((bf16[64,2,16,128]{3,2,1,0:T(8,128)(2,1)}), bf16[64,2,16,128]{3,2,1,0:T(8,128)(2,1)S(1)}, u32[]{:S(2)}, u32[]{:S(2)}) async-start(bf16[64,2,16,128]{3,2,1,0:T(8,128)(2,1)} %select_select_fusion), calls=%async_computation.1 | async-start | bytes 1048576 | tf_op jit(solution)/shard_map/all_to_all | solution.py:35
  44.0 0.1 fusion.21
  44.1 0.1 convert_add_fusion
  44.2 0.1 fusion.17
  44.4 16.4 %all-to-all-done.1 = bf16[64,2,16,128]{3,2,1,0:T(8,128)(2,1)S(1)} async-done(((bf16[64,2,16,128]{3,2,1,0:T(8,128)(2,1)}), bf16[64,2,16,128]{3,2,1,0:T(8,128)(2,1)S(1)}, u32[]{:S(2)}, u32[]{:S(2)}) %all-to-all-start.1) | async-done | bytes 524320 | tf_op jit(solution)/shard_map/all_to_all | solution.py:35
  60.9 0.4 fusion.3
  61.3 0.9 fusion.33
  62.2 0.1 copy.46
  62.3 0.6 fusion.10
  63.0 0.1 stack.3
  63.1 33.2 %all_to_all.15 = bf16[8,128,384]{1,2,0:T(8,128)(2,1)S(1)} all-to-all(bf16[8,128,384]{1,2,0:T(8,128)(2,1)S(1)} %stack.3), channel_id=1, replica_groups=mesh['req'=64,'tp'=8] {'tp'}, dimensions={0} | all-to-all | bytes 1572864 | tf_op jit(solution)/shard_map/all_to_all | solution.py:87
  96.3 3.6 %fusion.9 = bf16[1,128,640]{2,1,0:T(8,128)(2,1)} fusion(bf16[128,3072]{0,1:T(8,128)(2,1)S(1)} %bitcast.85, bf16[3072,640]{1,0:T(8,128)(2,1)} %param.21, bf16[1,128,640]{2,1,0:T(8,128)(2,1)S(1)} %copy-done), kind=kOutput, calls=%fused_computation.12 | convolution fusion | flops 503562240 | bytes 5046272 | tf_op jit(solution)/shard_map/dot_general | solution.py:88
  (31 shorter events, 0.5 us)
Async XLA Ops:
  1.1 15.0 %copy-start.3 = (s32[3]{0:T(128)S(1)}, s32[3]{0:T(128)}, u32[]{:S(2)}) copy-start(s32[3]{0:T(128)} %param.18) | copy-start | bytes 40
  1.1 19.4 %copy-start.5 = (bf16[2,128]{1,0:T(2,128)(2,1)S(1)}, bf16[2,128]{1,0:T(2,128)(2,1)}, u32[]{:S(2)}) copy-start(bf16[2,128]{1,0:T(2,128)(2,1)} %param.14) | copy-start | bytes 1540
  1.1 19.4 %copy-start.2 = (bf16[1,128,2,128]{3,2,1,0:T(2,128)(2,1)S(1)}, bf16[1,128,2,128]{3,2,1,0:T(2,128)(2,1)}, u32[]{:S(2)}) copy-start(bf16[1,128,2,128]{3,2,1,0:T(2,128)(2,1)} %param.12) | copy-start | bytes 196612
  1.1 19.6 %copy-start.1 = (bf16[1,128,384]{2,1,0:T(8,128)(2,1)S(1)}, bf16[1,128,384]{2,1,0:T(8,128)(2,1)}, u32[]{:S(2)}) copy-start(bf16[1,128,384]{2,1,0:T(8,128)(2,1)} %param.11) | copy-start | bytes 294916
  1.2 19.7 %copy-start.6 = (s32[1,128]{1,0:T(1,128)S(1)}, s32[1,128]{1,0:T(1,128)}, u32[]{:S(2)}) copy-start(s32[1,128]{1,0:T(1,128)} %param.19) | copy-start | bytes 1540
  2.4 21.7 %copy-start.4 = (bf16[384]{0:T(512)(128)(2,1)S(1)}, bf16[384]{0:T(512)(128)(2,1)}, u32[]{:S(2)}) copy-start(bf16[384]{0:T(512)(128)(2,1)} %param.13) | copy-start | bytes 2308
  3.6 30.9 %all-to-all-start = ((bf16[64,17,2,128]{3,2,1,0:T(2,128)(2,1)}), bf16[64,17,2,128]{3,2,1,0:T(2,128)(2,1)S(1)}, u32[]{:S(2)}, u32[]{:S(2)}) async-start(bf16[64,17,2,128]{3,2,1,0:T(2,128)(2,1)} %concatenate.45.clone), calls=%async_computation | async-start | bytes 1114112 | tf_op jit(solution)/shard_map/all_to_all | solution.py:26
  38.0 22.8 %all-to-all-start.1 = ((bf16[64,2,16,128]{3,2,1,0:T(8,128)(2,1)}), bf16[64,2,16,128]{3,2,1,0:T(8,128)(2,1)S(1)}, u32[]{:S(2)}, u32[]{:S(2)}) async-start(bf16[64,2,16,128]{3,2,1,0:T(8,128)(2,1)} %select_select_fusion), calls=%async_computation.1 | async-start | bytes 1048576 | tf_op jit(solution)/shard_map/all_to_all | solution.py:35
  63.0 33.4 %copy-start = (bf16[1,128,640]{2,1,0:T(8,128)(2,1)S(1)}, bf16[1,128,640]{2,1,0:T(8,128)(2,1)}, u32[]{:S(2)}) copy-start(bf16[1,128,640]{2,1,0:T(8,128)(2,1)} %param.20) | copy-start | bytes 491524
